TPU v7x, 256 devices: a whole 4x4x8 slice. The times are simulated.
256 devices in a mesh: row: 8 (over x_hi, y), col: 32 (over x_lo, z, core).
Axes of the slice: x: 4 (x_hi: 2, x_lo: 2; x = x_hi * 2 + x_lo), y: 4, z: 8, core: 2. Of those that a mesh axis runs over, the one named last changes fastest.
Arguments:
- orbitals: bfloat16 [16384, 1024], P('row', 'col'), may hold values from -0.1875 to 0.1875
- kernel: bfloat16 [16384, 16384], P('col', 'row'), may hold values from -6 to 6
- applied: bfloat16 [16384, 512], P('col', 'row'), may hold values from -1.5 to 1.5
- fit: bfloat16 [16384, 65536], P('row', 'col'), may hold values from -0.046875 to 0.046875
Outputs:
- exchange_term: bfloat16 [512, 65536], P('row', 'col')
All inputs are finite; a program needn't handle non-finite values.
Results may differ from a plain program's by a relative error of at most 0.0058.
Values may be sent and summed in bfloat16 or wider, within the bound.
No kernel may reach another device: no remote copies, remote signals or barrier semaphores. Data moves between devices by JAX's collectives and lax.ppermute only.
A program may use at most 64 MiB of HBM per device.

v0:
```python
import jax
import jax.numpy as jnp
from jax import lax
from jax.sharding import PartitionSpec as P


def per_device(orbitals, kernel, applied, fit):
    columns = lax.all_gather(orbitals, "row", axis=0, tiled=True)
    nearby = lax.all_to_all(columns, "col", split_axis=0, concat_axis=1, tiled=True)
    density = lax.dot_general(
        nearby,
        lax.all_gather(orbitals, "col", axis=1, tiled=True),
        (((1,), (1,)), ((), ())),
        preferred_element_type=jnp.float32,
    )
    weighted = (density * kernel.astype(jnp.float32)).astype(jnp.bfloat16)
    partial_sum = lax.dot_general(
        weighted,
        lax.all_gather(applied, "row", axis=1, tiled=True),
        (((0,), (0,)), ((), ())),
        preferred_element_type=jnp.float32,
    )
    projected = lax.psum(partial_sum, "col")
    projected_low = projected.astype(jnp.bfloat16)
    result = lax.psum_scatter(
        -lax.dot_general(
            projected_low, fit, (((0,), (0,)), ((), ())), preferred_element_type=jnp.float32
        ),
        "row",
        scatter_dimension=0,
        tiled=True,
    )
    return result.astype(jnp.bfloat16)


def solution(mesh):
    return jax.shard_map(
        per_device,
        mesh=mesh,
        in_specs=(P("row", "col"), P("col", "row"), P("col", "row"), P("row", "col")),
        out_specs=P("row", "col"),
        check_vma=False,
    )
```

profile of v0, /device:TPU:8, one launch (start us, length us, event | category | flops | bytes accessed | tf_op | source)
XLA Modules:
  0.0 383.5 jit_solution(3494709787726680160)
XLA Ops:
  6.5 0.0 copy-start
  6.5 0.0 all-gather.3.cloned.1.call-start
  6.5 0.7 all-gather.3.cloned.1.call-update
  7.3 0.0 all-gather.5.cloned.1.call-start
  7.3 0.7 all-gather.5.cloned.1.call-update
  8.0 55.9 %all-gather.3.cloned.1.call-done = bf16[16384,32]{0,1:T(8,128)(2,1)} async-done(((bf16[2048,32]{0,1:T(8,128)(2,1)}), bf16[16384,32]{0,1:T(8,128)(2,1)}) %all-gather.3.cloned.1.call-update) | async-done | bytes 1048592 | tf_op jit(solution)/shard_map/all_gather | solution.py:8
  63.9 2.4 copy.9
  66.3 7.4 %all-to-all-start = ((bf16[32,512,32]{1,2,0:T(8,128)(2,1)}), bf16[32,512,32]{1,2,0:T(8,128)(2,1)S(1)}, u32[]{:S(2)}, u32[]{:S(2)}) async-start(bf16[32,512,32]{1,2,0:T(8,128)(2,1)} %bitcast.11), calls=%async_computation | async-start | bytes 2097152 | tf_op jit(solution)/shard_map/all_to_all | solution.py:9
  73.7 0.0 reduce-scatter.2.cloned.1.call-start
  73.8 0.0 copy-done
  73.8 37.0 %all_gather.11 = bf16[512,512]{0,1:T(8,128)(2,1)S(1)} all-gather(bf16[512,64]{0,1:T(8,128)(2,1)S(1)} %copy-done), channel_id=1, replica_groups=mesh['row'=8,'col'=32] {'row'}, dimensions={1}, use_global_device_ids=true | all-gather | bytes 589824 | tf_op jit(solution)/shard_map/all_gather | solution.py:19
  110.8 0.0 all-to-all-done
  110.8 30.2 %all-gather.5.cloned.1.call-done = bf16[2048,1024]{0,1:T(8,128)(2,1)} async-done(((bf16[2048,32]{0,1:T(8,128)(2,1)}), bf16[2048,1024]{0,1:T(8,128)(2,1)}) %all-gather.5.cloned.1.call-update) | async-done | bytes 4194320 | tf_op jit(solution)/shard_map/all_gather | solution.py:12
  140.9 8.3 %fusion.1 = f32[2048,512]{1,0:T(8,128)} fusion(bf16[512,512]{0,1:T(8,128)(2,1)S(1)} %all_gather.11, bf16[512,2048]{1,0:T(8,128)(2,1)} %param.5, bf16[512,1024]{0,1:T(8,128)(2,1)S(1)} %bitcast.12, bf16[2048,1024]{0,1:T(8,128)(2,1)} %all-gather.5.cloned.1.call-done), kind=kOutput, calls=%fused_computation.3 | convolution fusion | flops 3224371200 | bytes 12058624 | tf_op jit(solution)/shard_map/dot_general | solution.py:17
  149.2 130.4 %all-reduce.1 = bf16[2048,512]{1,0:T(8,128)(2,1)S(1)} all-reduce(f32[2048,512]{1,0:T(8,128)} %fusion.1), channel_id=1, replica_groups=mesh['row'=8,'col'=32] {'col'}, use_global_device_ids=true, to_apply=%region_0.0 | all-reduce | flops 1048576 | bytes 6291456 | tf_op jit(solution)/shard_map/psum | solution.py:23
  279.7 9.5 %convolution_negate_fusion = f32[512,2048]{1,0:T(8,128)} fusion(bf16[2048,2048]{1,0:T(8,128)(2,1)} %param.7, bf16[2048,512]{1,0:T(8,128)(2,1)S(1)} %all-reduce.1), kind=kOutput, calls=%fused_computation.1 | convolution fusion | flops 4296015872 | bytes 14680064 | tf_op jit(solution)/shard_map/dot_general | solution.py:26
  289.1 0.0 reduce-scatter.2.cloned.1.call-update
  289.1 86.1 %reduce-scatter.2.cloned.1.call-done = f32[64,2048]{1,0:T(8,128)} async-done(((f32[512,2048]{1,0:T(8,128)}), f32[64,2048]{1,0:T(8,128)}) %reduce-scatter.2.cloned.1.call-update) | async-done | bytes 524304 | tf_op jit(solution)/shard_map/reduce_scatter | solution.py:25
  375.2 1.8 convert_element_type.15
Async XLA Ops:
  6.5 67.2 %copy-start = (bf16[512,64]{0,1:T(8,128)(2,1)S(1)}, bf16[512,64]{0,1:T(8,128)(2,1)}, u32[]{:S(2)}) copy-start(bf16[512,64]{0,1:T(8,128)(2,1)} %param.6) | copy-start | bytes 196612
  6.5 57.4 %all-gather.3.cloned.1.call-start = ((), (), s32[]{:S(2)}) async-start(), calls=%async_computation.2 | async-start | bytes 1179648 | tf_op jit(solution)/shard_map/all_gather | solution.py:8
  7.3 133.7 %all-gather.5.cloned.1.call-start = ((), (), s32[]{:S(2)}) async-start(), calls=%async_computation.3 | async-start | bytes 4325376 | tf_op jit(solution)/shard_map/all_gather | solution.py:12
  66.3 44.5 %all-to-all-start = ((bf16[32,512,32]{1,2,0:T(8,128)(2,1)}), bf16[32,512,32]{1,2,0:T(8,128)(2,1)S(1)}, u32[]{:S(2)}, u32[]{:S(2)}) async-start(bf16[32,512,32]{1,2,0:T(8,128)(2,1)} %bitcast.11), calls=%async_computation | async-start | bytes 2097152 | tf_op jit(solution)/shard_map/all_to_all | solution.py:9
  73.7 301.5 %reduce-scatter.2.cloned.1.call-start = ((), (), s32[]{:S(2)}) async-start(), calls=%async_computation.4 | async-start | bytes 4718592 | tf_op jit(solution)/shard_map/reduce_scatter | solution.py:25
Sparse Core Ops, SparseCore 0:
  9.9 53.9 all-gather.2
  65.8 75.0 all-gather.4
  289.3 85.8 reduce-scatter.1
where the time goes:
time: 384 us
  waiting for transfers between devices  174 us (45%)
  blocking collectives  167 us (43%)
  matrix products  17.8 us (5%)
  between operations  13.1 us (3%)
  starting transfers between devices  7.49 us (2%)
    psum x1, blocking collectives, per_device(): projected = lax.psum(partial_sum, 'col')  130 us
    reduce_scatter x1, waiting for transfers between devices, per_device(): lax.psum_scatter(-lax.dot_general(projected_low, fit, (((0,), (0,)), ((),...  86.1 us
    all_gather x1, waiting for transfers between devices, per_device(): columns = lax.all_gather(orbitals, 'row', axis=0, tiled=True)  55.9 us
    all_gather x1, blocking collectives, per_device(): lax.all_gather(applied, 'row', axis=1, tiled=True)  37 us
    all_gather x1, waiting for transfers between devices, per_device(): lax.all_gather(orbitals, 'col', axis=1, tiled=True)  30.2 us
    dot_general x1, matrix products, per_device(): lax.dot_general(projected_low, fit, (((0,), (0,)), ((), ())), preferred_e...  9.47 us
    dot_general x1, matrix products, per_device(): lax.dot_general(weighted, lax.all_gather(applied, 'row', axis=1, tiled=Tr...  8.31 us
  transfers between devices with their start and end apart: 4, of which 3 were waited for; matrix products, arithmetic and copies ran while one was open for 1% of the time, Pallas kernels for 0%

commit v1 on v0

--- a/solution.py
+++ b/solution.py
@@ -9,7 +9,7 @@
     nearby = lax.all_to_all(columns, "col", split_axis=0, concat_axis=1, tiled=True)
     density = lax.dot_general(
         nearby,
-        lax.all_gather(orbitals, "col", axis=1, tiled=True),
+        jnp.concatenate(lax.all_gather(orbitals, "col"), axis=1),
         (((1,), (1,)), ((), ())),
         preferred_element_type=jnp.float32,
     )

time: 384 us -> 384 us (level)
  no operation moved by 1% of the time
where the time goes in v1:
time: 384 us
  waiting for transfers between devices  173 us (45%)
  blocking collectives  168 us (44%)
  matrix products  17.8 us (5%)
  between operations  13.1 us (3%)
  starting transfers between devices  7.49 us (2%)
    psum x1, blocking collectives, per_device(): projected = lax.psum(partial_sum, 'col')  131 us
    reduce_scatter x1, waiting for transfers between devices, per_device(): lax.psum_scatter(-lax.dot_general(projected_low, fit, (((0,), (0,)), ((),...  86 us
    all_gather x1, waiting for transfers between devices, per_device(): columns = lax.all_gather(orbitals, 'row', axis=0, tiled=True)  55.9 us
    all_gather x1, blocking collectives, per_device(): lax.all_gather(applied, 'row', axis=1, tiled=True)  37 us
    all_gather x1, waiting for transfers between devices, per_device(): lax.all_gather(orbitals, 'col')  29.6 us
    dot_general x1, matrix products, per_device(): lax.dot_general(projected_low, fit, (((0,), (0,)), ((), ())), preferred_e...  9.47 us
    dot_general x1, matrix products, per_device(): lax.dot_general(weighted, lax.all_gather(applied, 'row', axis=1, tiled=Tr...  8.31 us
  transfers between devices with their start and end apart: 4, of which 3 were waited for; matrix products, arithmetic and copies ran while one was open for 1% of the time, Pallas kernels for 0%

profile of v1, /device:TPU:8, one launch (start us, length us, event | category | flops | bytes accessed | tf_op | source)
XLA Modules:
  0.0 383.6 jit_solution(8756597050277939516)
XLA Ops:
  6.5 0.0 copy-start
  6.5 0.0 all-gather.4.cloned.1.call-start
  6.5 0.7 all-gather.4.cloned.1.call-update
  7.3 0.0 all-gather.6.cloned.1.call-start
  7.3 0.7 all-gather.6.cloned.1.call-update
  8.0 55.9 %all-gather.4.cloned.1.call-done = bf16[16384,32]{0,1:T(8,128)(2,1)} async-done(((bf16[2048,32]{0,1:T(8,128)(2,1)}), bf16[16384,32]{0,1:T(8,128)(2,1)}) %all-gather.4.cloned.1.call-update) | async-done | bytes 1048592 | tf_op jit(solution)/shard_map/all_gather | solution.py:8
  63.9 2.4 copy.19
  66.3 7.4 %all-to-all-start = ((bf16[32,512,32]{1,2,0:T(8,128)(2,1)}), bf16[32,512,32]{1,2,0:T(8,128)(2,1)S(1)}, u32[]{:S(2)}, u32[]{:S(2)}) async-start(bf16[32,512,32]{1,2,0:T(8,128)(2,1)} %bitcast.31), calls=%async_computation | async-start | bytes 2097152 | tf_op jit(solution)/shard_map/all_to_all | solution.py:9
  73.7 0.0 reduce-scatter.2.cloned.1.call-start
  73.8 0.0 copy-done
  73.8 37.0 %all_gather.15 = bf16[512,512]{0,1:T(8,128)(2,1)S(1)} all-gather(bf16[512,64]{0,1:T(8,128)(2,1)S(1)} %copy-done), channel_id=1, replica_groups=mesh['row'=8,'col'=32] {'row'}, dimensions={1}, use_global_device_ids=true | all-gather | bytes 589824 | tf_op jit(solution)/shard_map/all_gather | solution.py:19
  110.8 0.0 all-to-all-done
  110.8 29.6 %all-gather.6.cloned.1.call-done = bf16[65536,32]{0,1:T(8,128)(2,1)} async-done(((bf16[2048,32]{0,1:T(8,128)(2,1)}), bf16[65536,32]{0,1:T(8,128)(2,1)}) %all-gather.6.cloned.1.call-update) | async-done | bytes 4194320 | tf_op jit(solution)/shard_map/all_gather | solution.py:12
  140.3 8.3 %fusion.4 = f32[2048,512]{1,0:T(8,128)} fusion(bf16[512,512]{0,1:T(8,128)(2,1)S(1)} %all_gather.15, bf16[512,2048]{1,0:T(8,128)(2,1)} %param.5, bf16[4,32,8,2048]{3,2,1,0:T(8,128)(2,1)} %bitcast.33, bf16[32,512,32]{1,2,0:T(8,128)(2,1)S(1)} %all-to-all-done), kind=kOutput, calls=%fused_computation.7 | convolution fusion | flops 3224371200 | bytes 12058624 | tf_op jit(solution)/shard_map/dot_general | solution.py:17
  148.6 131.1 %all-reduce.1 = bf16[2048,512]{1,0:T(8,128)(2,1)S(1)} all-reduce(f32[2048,512]{1,0:T(8,128)} %fusion.4), channel_id=1, replica_groups=mesh['row'=8,'col'=32] {'col'}, use_global_device_ids=true, to_apply=%region_0.0 | all-reduce | flops 1048576 | bytes 6291456 | tf_op jit(solution)/shard_map/psum | solution.py:23
  279.8 9.5 %convolution_negate_fusion = f32[512,2048]{1,0:T(8,128)} fusion(bf16[2048,2048]{1,0:T(8,128)(2,1)} %param.7, bf16[2048,512]{1,0:T(8,128)(2,1)S(1)} %all-reduce.1), kind=kOutput, calls=%fused_computation.5 | convolution fusion | flops 4296015872 | bytes 14680064 | tf_op jit(solution)/shard_map/dot_general | solution.py:26
  289.3 0.0 reduce-scatter.2.cloned.1.call-update
  289.3 86.0 %reduce-scatter.2.cloned.1.call-done = f32[64,2048]{1,0:T(8,128)} async-done(((f32[512,2048]{1,0:T(8,128)}), f32[64,2048]{1,0:T(8,128)}) %reduce-scatter.2.cloned.1.call-update) | async-done | bytes 524304 | tf_op jit(solution)/shard_map/reduce_scatter | solution.py:25
  375.2 1.8 convert_element_type.15
Async XLA Ops:
  6.5 67.2 %copy-start = (bf16[512,64]{0,1:T(8,128)(2,1)S(1)}, bf16[512,64]{0,1:T(8,128)(2,1)}, u32[]{:S(2)}) copy-start(bf16[512,64]{0,1:T(8,128)(2,1)} %param.6) | copy-start | bytes 196612
  6.5 57.4 %all-gather.4.cloned.1.call-start = ((), (), s32[]{:S(2)}) async-start(), calls=%async_computation.2 | async-start | bytes 1179648 | tf_op jit(solution)/shard_map/all_gather | solution.py:8
  7.3 133.1 %all-gather.6.cloned.1.call-start = ((), (), s32[]{:S(2)}) async-start(), calls=%async_computation.4 | async-start | bytes 4325376 | tf_op jit(solution)/shard_map/all_gather | solution.py:12
  66.3 44.5 %all-to-all-start = ((bf16[32,512,32]{1,2,0:T(8,128)(2,1)}), bf16[32,512,32]{1,2,0:T(8,128)(2,1)S(1)}, u32[]{:S(2)}, u32[]{:S(2)}) async-start(bf16[32,512,32]{1,2,0:T(8,128)(2,1)} %bitcast.31), calls=%async_computation | async-start | bytes 2097152 | tf_op jit(solution)/shard_map/all_to_all | solution.py:9
  73.7 301.5 %reduce-scatter.2.cloned.1.call-start = ((), (), s32[]{:S(2)}) async-start(), calls=%async_computation.3 | async-start | bytes 4718592 | tf_op jit(solution)/shard_map/reduce_scatter | solution.py:25
Sparse Core Ops, SparseCore 0:
  9.9 53.9 all-gather.3
  65.8 74.4 all-gather.5
  289.4 85.7 reduce-scatter.1
